TPU v7x, 32 devices: a whole 2x2x4 slice. The times are simulated.
32 devices in a mesh: chan: 8 (over z, x), tm: 4 (over y, core).
Axes of the slice: x: 2, y: 2, z: 4, core: 2. Of those that a mesh axis runs over, the one named last changes fastest.
Arguments:
- samples: bfloat16 [2048, 131072], P('chan', 'tm'), may hold values from -6 to 6
- fir_taps: float32 [8, 4096], replicated, may hold values from -2 to 2
- beam_y: bfloat16 [2, 32, 32], replicated, may hold values from -0.75 to 0.75
- beam_x: bfloat16 [2, 64, 64], replicated, may hold values from -0.5 to 0.5
- delays: int32 [64, 2048], replicated, may hold values from 0 to 8, as said below
Outputs:
- series: float32 [2048, 32, 64], P('chan', 'tm')
Inputs may be any that keep to these rules, and one draw needn't show every extreme that they name: Each trial's delays come from a dispersion law: along a row they never rise with the channel index; the largest value is reached.
All inputs are finite; a program needn't handle non-finite values.
Results may differ from a plain program's by a relative error of at most 0.00068.
Values may be sent and summed in bfloat16 or wider, within the bound.
No kernel may reach another device: no remote copies, remote signals or barrier semaphores. Data moves between devices by JAX's collectives and lax.ppermute only.
A program may use at most 192 MiB of HBM per device.

v0:
```python
import math
import jax
import jax.numpy as jnp
from jax import lax
from jax.sharding import PartitionSpec as P


def shifted(array, axis, by):
    count = lax.axis_size(axis)
    pairs = [(i, i + by) for i in range(count) if 0 <= i + by < count]
    return lax.ppermute(array, axis, pairs)


def phase_table(rows_count, cols_count, period):
    row_index = jnp.arange(rows_count, dtype=jnp.int32)[:, None]
    col_index = jnp.arange(cols_count, dtype=jnp.int32)[None, :]
    angle = (row_index * col_index % period).astype(jnp.float32) * (2.0 * math.pi / period)
    return (jnp.cos(angle), jnp.sin(angle))


def transform(frames_rows, nfft):
    bits = nfft.bit_length() - 1
    first = 1 << bits // 2
    second = nfft // first
    rows_count = frames_rows.shape[0]
    shaped = frames_rows.reshape(rows_count, first, second)
    highest = lax.Precision.HIGHEST
    cos_one, sin_one = phase_table(first, first, first)
    section_real = jnp.einsum("rab,ak->rkb", shaped, cos_one, precision=highest)
    section_imag = -jnp.einsum("rab,ak->rkb", shaped, sin_one, precision=highest)
    cos_twist, sin_twist = phase_table(first, second, nfft)
    twist_real = section_real * cos_twist[None] + section_imag * sin_twist[None]
    twist_imag = section_imag * cos_twist[None] - section_real * sin_twist[None]
    cos_two, sin_two = phase_table(second, second // 2, second)
    out_real = jnp.einsum("rkb,bm->rmk", twist_real, cos_two, precision=highest) + jnp.einsum(
        "rkb,bm->rmk", twist_imag, sin_two, precision=highest
    )
    out_imag = jnp.einsum("rkb,bm->rmk", twist_imag, cos_two, precision=highest) - jnp.einsum(
        "rkb,bm->rmk", twist_real, sin_two, precision=highest
    )
    scale = 1.0 / math.sqrt(nfft)
    return (
        out_real.reshape(rows_count, nfft // 2) * scale,
        out_imag.reshape(rows_count, nfft // 2) * scale,
    )


def complex_product(weights, real_part, imag_part, form):
    w_real = weights[0]
    w_imag = weights[1]
    out_real = jnp.einsum(form, w_real, real_part, preferred_element_type=jnp.float32) - jnp.einsum(
        form, w_imag, imag_part, preferred_element_type=jnp.float32
    )
    out_imag = jnp.einsum(form, w_real, imag_part, preferred_element_type=jnp.float32) + jnp.einsum(
        form, w_imag, real_part, preferred_element_type=jnp.float32
    )
    return (out_real, out_imag)


def dedisperse(extended, delay_block, spec_dev, trials, scale):
    beam_count = extended.shape[2]

    def turn(shift_value, total):
        piece = lax.dynamic_slice_in_dim(extended, shift_value, spec_dev, 0)
        selector = (delay_block == shift_value).astype(jnp.bfloat16)
        return total + jnp.einsum(
            "scb,tc->bst", piece, selector, preferred_element_type=jnp.float32
        )

    summed = lax.fori_loop(
        0, spec_dev + 1, turn, jnp.zeros((beam_count, spec_dev, trials), jnp.float32)
    )
    return summed * scale


def on_device(samples, fir_taps, beam_y, beam_x, delays):
    dish_dev, total_points = samples.shape
    taps_count, nfft = fir_taps.shape
    spec_dev = total_points // nfft
    side_x = beam_x.shape[1]
    side_y = beam_y.shape[1]
    trials, channels = delays.shape
    frames = samples.reshape(dish_dev, spec_dev, nfft)
    history = shifted(frames[:, spec_dev - taps_count + 1 :, :], "tm", 1)
    extended_frames = jnp.concatenate([history, frames], axis=1)
    filtered = jnp.zeros((dish_dev, spec_dev, nfft), jnp.float32)
    for tap_index in range(taps_count):
        offset = taps_count - 1 - tap_index
        filtered = filtered + fir_taps[tap_index][None, None, :] * extended_frames[
            :, offset : offset + spec_dev, :
        ].astype(jnp.float32)
    frame_rows = filtered.reshape(dish_dev * spec_dev, nfft)
    volt_real, volt_imag = transform(frame_rows, nfft)
    volts = jnp.stack(
        [
            volt_real.reshape(dish_dev, spec_dev, nfft // 2),
            volt_imag.reshape(dish_dev, spec_dev, nfft // 2),
        ],
        axis=2,
    ).astype(jnp.bfloat16)
    gathered = lax.all_to_all(volts, "chan", split_axis=3, concat_axis=0, tiled=True)
    items = gathered.shape[1]
    chan_dev = gathered.shape[3]
    grid = gathered.reshape(side_x, side_y, items, 2, chan_dev)
    part_real, part_imag = complex_product(
        beam_y, grid[:, :, :, 0], grid[:, :, :, 1], "py,xync->ncxp"
    )
    part_real = part_real.astype(jnp.bfloat16)
    part_imag = part_imag.astype(jnp.bfloat16)
    form_real, form_imag = complex_product(beam_x, part_real, part_imag, "qx,ncxp->ncqp")
    power = (form_real * form_real + form_imag * form_imag).reshape(
        items, chan_dev, side_x * side_y
    )
    powers = (power - jnp.mean(power, axis=2, keepdims=True)).astype(jnp.bfloat16)
    scale = 1.0 / math.sqrt(channels)
    chan_dev = powers.shape[1]
    following = shifted(powers, "tm", -1)
    extended = jnp.concatenate([powers, following], axis=0)
    local_delays = lax.dynamic_slice_in_dim(delays, lax.axis_index("chan") * chan_dev, chan_dev, 1)
    return lax.psum_scatter(
        dedisperse(extended, local_delays, spec_dev, trials, scale),
        "chan",
        scatter_dimension=0,
        tiled=True,
    )


def solution(mesh):
    return jax.shard_map(
        on_device,
        mesh=mesh,
        in_specs=(P("chan", "tm"), P(), P(), P(), P()),
        out_specs=P("chan", "tm", None),
        check_vma=False,
    )
```

profile of v0, /device:TPU:0, one launch (start us, length us, event | category | flops | bytes accessed | tf_op | source)
XLA Modules:
  0.0 1550.4 jit_solution(6742614575479663688)
XLA Ops:
  6.5 22.5 %copy.72 = bf16[256,32768]{0,1:T(8,128)(2,1)} copy(bf16[256,32768]{1,0:T(8,128)(2,1)} %param.7) | data formatting | bytes 33554432 | tf_op args[0]
  29.0 13.1 slice.88
  42.1 19.4 %copy.73 = bf16[256,7,4096]{2,0,1:T(8,128)(2,1)} copy(bf16[256,7,4096]{0,2,1:T(8,128)(2,1)} %slice.88) | data formatting | bytes 29360128 | tf_op jit(solution)/shard_map/slice | solution.py:84
  61.5 7.5 collective-permute-start
  69.3 16.7 %collective-permute-done = bf16[256,7,4096]{2,0,1:T(8,128)(2,1)} collective-permute-done((bf16[256,7,4096]{2,0,1:T(8,128)(2,1)}, bf16[256,7,4096]{2,0,1:T(8,128)(2,1)}, u32[]{:S(2)}, u32[]{:S(2)}) %collective-permute-start) | collective-permute-done | bytes 14680096 | tf_op jit(solution)/shard_map/ppermute | solution.py:11
  86.0 19.3 %copy.74 = bf16[256,7,4096]{0,2,1:T(8,128)(2,1)} copy(bf16[256,7,4096]{2,0,1:T(8,128)(2,1)} %collective-permute-done) | data formatting | bytes 29360128 | tf_op jit(solution)/shard_map/ppermute | solution.py:11
  105.4 53.0 %multiply_add_fusion = f32[256,8,4096]{0,2,1:T(8,128)} fusion(bf16[256,8,4096]{0,2,1:T(8,128)(2,1)} %bitcast.115, bf16[256,7,4096]{0,2,1:T(8,128)(2,1)} %copy.74, f32[4096]{0:T(1024)S(1)} %bitcast.124, f32[4096]{0:T(1024)S(1)} %bitcast.125, f32[4096]{0:T(1024)S(1)} %bitcast.119, f32[4096]{0:T(1024)S(1)} %bitcast.120, f32[4096]{0:T(1024)S(1)} %bitcast.121, ...), kind=kLoop, calls=%fused_computation.21 | loop fusion | flops 251658240 | bytes 65142784 | tf_op jit(solution)/shard_map/add | solution.py:89
  158.4 31.9 %copy.75 = f32[256,8,4096]{2,1,0:T(8,128)} copy(f32[256,8,4096]{0,2,1:T(8,128)} %multiply_add_fusion) | data formatting | bytes 67108864 | tf_op jit(solution)/shard_map/add | solution.py:89
  190.3 52.7 %reshape_reshape.3 = f32[2048,64,64]{2,1,0:T(8,128)} reshape(f32[256,8,4096]{2,1,0:T(8,128)} %copy.75) | data formatting | bytes 67108864 | tf_op jit(solution)/shard_map/reshape;reshape | solution.py:26
  243.0 50.9 %copy.76 = f32[2048,64,64]{0,1,2:T(8,128)} copy(f32[2048,64,64]{2,1,0:T(8,128)} %reshape_reshape.3) | data formatting | bytes 67108864 | tf_op jit(solution)/shard_map/reshape;reshape | solution.py:26
  293.9 37.2 %fusion.44 = f32[64,2048,64]{1,0,2:T(8,128)} fusion(f32[2048,64,64]{0,1,2:T(8,128)} %copy.76), kind=kOutput, calls=%fused_computation.71 | convolution fusion | flops 6442508288 | bytes 67108864 | tf_op jit(solution)/shard_map/rab,ak->rkb/dot_general | solution.py:30
  331.1 55.2 %add_bitcast_fusion = (f32[2048,64,64]{0,1,2:T(8,128)}, f32[2048,64,64]{0,1,2:T(8,128)}) fusion(f32[64,2048,64]{1,0,2:T(8,128)} %fusion.44, f32[64,64]{0,1:T(8,128)S(1)} %get-tuple-element.138, f32[64,64]{0,1:T(8,128)S(1)} %get-tuple-element.139, f32[2048,64,64]{0,1,2:T(8,128)} %copy.76), kind=kOutput, calls=%fused_computation.20 | convolution fusion | flops 6501228544 | bytes 134250496 | tf_op jit(solution)/shard_map/rab,ak->rkb/dot_general | solution.py:29
  386.3 45.7 %fusion.10 = f32[32,2048,64]{1,0,2:T(8,128)} fusion(f32[2048,64,64]{0,1,2:T(8,128)} %get-tuple-element.125), kind=kOutput, calls=%fused_computation.24 | convolution fusion | flops 3221254144 | bytes 50331648 | tf_op jit(solution)/shard_map/rkb,bm->rmk/dot_general | solution.py:35
  432.0 46.2 %fusion.8 = f32[32,2048,64]{1,0,2:T(8,128)} fusion(f32[2048,64,64]{0,1,2:T(8,128)} %get-tuple-element.125), kind=kOutput, calls=%fused_computation.22 | convolution fusion | flops 3221254144 | bytes 50331648 | tf_op jit(solution)/shard_map/rkb,bm->rmk/dot_general | solution.py:38
  478.2 49.5 %fusion.23 = bf16[2048,32,64]{0,1,2:T(8,128)(2,1)} fusion(f32[32,2048,64]{1,0,2:T(8,128)} %fusion.10, f32[2048,64,64]{0,1,2:T(8,128)} %get-tuple-element.124), kind=kOutput, calls=%fused_computation.46 | convolution fusion | flops 3233837056 | bytes 58720256 | tf_op jit(solution)/shard_map/rkb,bm->rmk/dot_general | solution.py:35
  527.7 29.2 %copy.80 = bf16[2048,32,64]{2,1,0:T(8,128)(2,1)} copy(bf16[2048,32,64]{0,1,2:T(8,128)(2,1)} %fusion.23) | data formatting | bytes 16777216 | tf_op jit(solution)/shard_map/mul | solution.py:43
  556.9 23.4 %mul.337 = bf16[256,8,1,2048]{3,1,0,2:T(8,128)(2,1)} reshape(bf16[2048,32,64]{2,1,0:T(8,128)(2,1)} %copy.80) | data formatting | bytes 16777216 | tf_op jit(solution)/shard_map/mul | solution.py:43
  580.4 48.1 %fusion.24 = bf16[2048,32,64]{0,1,2:T(8,128)(2,1)} fusion(f32[32,2048,64]{1,0,2:T(8,128)} %fusion.8, f32[2048,64,64]{0,1,2:T(8,128)} %get-tuple-element.124), kind=kOutput, calls=%fused_computation.47 | convolution fusion | flops 3233837056 | bytes 58720256 | tf_op jit(solution)/shard_map/rkb,bm->rmk/dot_general | solution.py:38
  628.5 29.4 %copy.83 = bf16[2048,32,64]{2,1,0:T(8,128)(2,1)} copy(bf16[2048,32,64]{0,1,2:T(8,128)(2,1)} %fusion.24) | data formatting | bytes 16777216 | tf_op jit(solution)/shard_map/mul | solution.py:44
  657.9 23.4 %mul.340 = bf16[256,8,1,2048]{3,1,0,2:T(8,128)(2,1)} reshape(bf16[2048,32,64]{2,1,0:T(8,128)(2,1)} %copy.83) | data formatting | bytes 16777216 | tf_op jit(solution)/shard_map/mul | solution.py:44
  681.3 13.7 pad_maximum_fusion.1
  695.1 25.6 %copy.84 = bf16[256,8,2,2048]{0,1,2,3:T(8,128)(2,1)} copy(bf16[256,8,2,2048]{3,1,0,2:T(8,128)(2,1)} %pad_maximum_fusion.1) | data formatting | bytes 33554432 | tf_op jit(solution)/shard_map/stack | solution.py:94
  720.6 324.9 %all_to_all.15 = bf16[256,8,2,2048]{0,1,2,3:T(8,128)(2,1)} all-to-all(bf16[256,8,2,2048]{0,1,2,3:T(8,128)(2,1)} %copy.84), channel_id=1, replica_groups=mesh['chan'=8,'tm'=4] {'chan'}, dimensions={3} | all-to-all | bytes 33554432 | tf_op jit(solution)/shard_map/all_to_all | solution.py:101
  1045.5 25.7 %copy.86 = bf16[8,256,8,2,256]{4,2,3,1,0:T(8,128)(2,1)} copy(bf16[8,256,8,2,256]{1,2,3,4,0:T(8,128)(2,1)} %bitcast.117) | data formatting | bytes 33554432 | tf_op jit(solution)/shard_map/all_to_all | solution.py:101
  1071.3 6.6 fusion.117
  1081.1 8.1 fusion.25
  1089.2 8.1 fusion.26
  1097.2 13.8 fusion.39
  1111.0 16.0 %fusion.27 = f32[8,256,32,64]{1,3,2,0:T(8,128)} fusion(bf16[8,256,64,32]{1,3,0,2:T(8,128)(2,1)} %fusion.39, bf16[2,64,64]{2,1,0:T(8,128)(2,1)S(1)} %copy-done.6), kind=kOutput, calls=%fused_computation.52 | convolution fusion | flops 536870912 | bytes 25182208 | tf_op jit(solution)/shard_map/qx,ncxp->ncqp/dot_general | solution.py:51
  1127.0 12.3 fusion.29
  1139.2 13.7 fusion.38
  1153.0 16.0 %fusion.31 = f32[8,256,32,64]{1,3,2,0:T(8,128)} fusion(bf16[8,256,64,32]{1,3,0,2:T(8,128)(2,1)} %fusion.38, bf16[2,64,64]{2,1,0:T(8,128)(2,1)S(1)} %copy-done.6), kind=kOutput, calls=%fused_computation.56 | convolution fusion | flops 536870912 | bytes 25182208 | tf_op jit(solution)/shard_map/qx,ncxp->ncqp/dot_general | solution.py:51
  1169.0 23.3 %fusion.119 = (f32[8,256]{1,0:T(8,128)S(1)}, f32[8,256,64,32]{1,2,3,0:T(8,128)}) fusion(f32[8,256,32,64]{1,3,2,0:T(8,128)} %fusion.29, bf16[8,256,64,32]{1,3,0,2:T(8,128)(2,1)S(1)} %copy-done.4, bf16[2,64,64]{2,1,0:T(8,128)(2,1)S(1)} %copy-done.6, f32[8,256,32,64]{1,3,2,0:T(8,128)} %fusion.31, f32[8,256,32,64]{1,3,2,0:T(8,128)} %fusion.27), kind=kOutput, calls=%fused_computation.146 | convolution fusion | flops 562034688 | bytes 75522048 | tf_op jit(solution)/shard_map/qx,ncxp->ncqp/dot_general | solution.py:54
  1192.3 15.2 copy.93
  1207.5 4.9 fusion.22
  1213.8 60.9 %collective-permute-done.1 = bf16[8,256,2048]{1,2,0:T(8,128)(2,1)} collective-permute-done((bf16[8,256,2048]{1,2,0:T(8,128)(2,1)}, bf16[8,256,2048]{1,2,0:T(8,128)(2,1)}, u32[]{:S(2)}, u32[]{:S(2)}) %collective-permute-start.1) | collective-permute-done | bytes 8388640 | tf_op jit(solution)/shard_map/ppermute | solution.py:11
  1274.6 13.7 pad_maximum_fusion.2
  1288.3 82.9 %while.14 = (s32[]{:T(128)}, f32[2048,8,64]{0,2,1:T(8,128)}, s32[64,256]{1,0:T(8,128)S(1)}, bf16[16,256,2048]{1,2,0:T(8,128)(2,1)}, s32[]{:T(128)}, /*index=5*/s32[]{:T(128)}) while((s32[]{:T(128)}, f32[2048,8,64]{0,2,1:T(8,128)}, s32[64,256]{1,0:T(8,128)S(1)}, bf16[16,256,2048]{1,2,0:T(8,128)(2,1)}, s32[]{:T(128)}, ...), condition=%wide.region_2.3_spmd.clone, body=%wide.region_1.2_spmd.clone.sunk | while | flops 538984448 | bytes 16843852 | solution.py:70
  1288.3 8.1 bitcast_add_fusion.2
  1296.4 9.5 bitcast_add_fusion.2
  1305.9 9.5 bitcast_add_fusion.2
  1315.4 9.5 bitcast_add_fusion.2
  1324.8 9.3 bitcast_add_fusion.2
  1334.1 9.3 bitcast_add_fusion.2
  1343.4 9.3 bitcast_add_fusion.2
  1352.7 9.3 bitcast_add_fusion.2
  1361.9 9.3 bitcast_add_fusion.2
  1376.1 167.2 %reduce-scatter.2.cloned.1.call-done = f32[256,8,64]{0,2,1:T(8,128)} async-done(((f32[2048,8,64]{0,2,1:T(8,128)}), f32[256,8,64]{0,2,1:T(8,128)}) %reduce-scatter.2.cloned.1.call-update) | async-done | bytes 524304 | tf_op jit(solution)/shard_map/reduce_scatter | solution.py:120
  (25 shorter events, 9.7 us)
Async XLA Ops:
  6.5 1207.2 %copy-start = (s32[64,2048]{1,0:T(8,128)S(1)}, s32[64,2048]{1,0:T(8,128)}, u32[]{:S(2)}) copy-start(s32[64,2048]{1,0:T(8,128)} %param.11) | copy-start | bytes 1572868
  6.5 1536.8 %reduce-scatter.2.cloned.1.call-start = ((), (), s32[]{:S(2)}) async-start(), calls=%async_computation.2 | async-start | bytes 4718592 | tf_op jit(solution)/shard_map/reduce_scatter | solution.py:120
  42.1 27.1 %copy-start.5 = (f32[8,4096]{1,0:T(8,128)S(1)}, f32[8,4096]{1,0:T(8,128)}, u32[]{:S(2)}) copy-start(f32[8,4096]{1,0:T(8,128)} %param.8) | copy-start | bytes 393220
  61.5 24.5 %collective-permute-start = (bf16[256,7,4096]{2,0,1:T(8,128)(2,1)}, bf16[256,7,4096]{2,0,1:T(8,128)(2,1)}, u32[]{:S(2)}, u32[]{:S(2)}) collective-permute-start(bf16[256,7,4096]{2,0,1:T(8,128)(2,1)} %copy.73), channel_id=1, source_target_pairs={{0,1},{1,2},{2,3},{4,5},{5,6},{6,7},{8,9},{9,10},{10,11},{12,13},{... | collective-permute-start | bytes 44040200 | tf_op jit(solution)/shard_map/ppermute | solution.py:11
  1071.3 9.8 copy-start.7
  1077.9 3.2 copy-start.2
  1077.9 11.3 copy-start.1
  1097.2 13.8 copy-start.6
  1111.0 16.0 %copy-start.3 = (bf16[8,256,64,32]{1,3,0,2:T(8,128)(2,1)S(1)}, bf16[8,256,64,32]{1,3,0,2:T(8,128)(2,1)}, u32[]{:S(2)}) copy-start(bf16[8,256,64,32]{1,3,0,2:T(8,128)(2,1)} %fusion.39) | copy-start | bytes 25165828
  1153.0 16.0 %copy-start.4 = (bf16[8,256,64,32]{1,3,0,2:T(8,128)(2,1)S(1)}, bf16[8,256,64,32]{1,3,0,2:T(8,128)(2,1)}, u32[]{:S(2)}) copy-start(bf16[8,256,64,32]{1,3,0,2:T(8,128)(2,1)} %fusion.38) | copy-start | bytes 25165828
  1212.4 62.2 %collective-permute-start.1 = (bf16[8,256,2048]{1,2,0:T(8,128)(2,1)}, bf16[8,256,2048]{1,2,0:T(8,128)(2,1)}, u32[]{:S(2)}, u32[]{:S(2)}) collective-permute-start(bf16[8,256,2048]{1,2,0:T(8,128)(2,1)} %fusion.22), channel_id=1, source_target_pairs={{1,0},{2,1},{3,2},{5,4},{6,5},{7,6},{9,8},{10,9},{11,10},{13,12},{... | collective-permute-start | bytes 25165832 | tf_op jit(solution)/shard_map/ppermute | solution.py:11
Sparse Core Ops, SparseCore 0:
  1376.2 166.9 reduce-scatter.1
where the time goes:
time: 1560 us; the launch traced here: 1550 us
  matrix products  476 us (31%)
  local copies, waits for them, and re-layouts  392 us (25%)
  blocking collectives  325 us (21%)
  waiting for transfers between devices  245 us (16%)
  other arithmetic  90.4 us (6%)
    all_to_all x1, blocking collectives, on_device(): lax.all_to_all(volts, 'chan', split_axis=3, concat_axis=0, tiled=True)  325 us
    reduce_scatter x1, waiting for transfers between devices, on_device(): lax.psum_scatter(dedisperse(extended, local_delays, spec_dev, trials, sca...  167 us
    another operation x2, local copies, waits for them, and re-layouts, transform(): shaped = frames_rows.reshape(rows_count, first, second)  104 us
    dot_general x9, matrix products, turn(): jnp.einsum('scb,tc->bst', piece, selector, preferred_element_type=jnp.flo...  82.9 us
    ppermute x2, waiting for transfers between devices, shifted(): return lax.ppermute(array, axis, pairs)  77.6 us
    dot_general x1, matrix products, transform(): section_real = jnp.einsum('rab,ak->rkb', shaped, cos_one, precision=highest)  55.2 us
    add x1, other arithmetic, on_device(): filtered + fir_taps[tap_index][None, None, :] * extended_frames[:, offset...  53 us
    mul x2, local copies, waits for them, and re-layouts, transform(): out_imag.reshape(rows_count, nfft // 2) * scale  52.9 us
  transfers between devices with their start and end apart: 3, of which 3 were waited for; matrix products, arithmetic and copies ran while one was open for 0% of the time, Pallas kernels for 0%

commit v1 on v0

--- a/solution.py
+++ b/solution.py
@@ -3,6 +3,18 @@
 import jax.numpy as jnp
 from jax import lax
 from jax.sharding import PartitionSpec as P
+
+
+def sectors_trace(u, on_dim, arr):
+    tall, low = (u.shape[:on_dim], u.shape[on_dim + 1 :])
+    u_next = u.reshape(*tall, arr, -1, *low)
+    return jnp.moveaxis(u_next, on_dim, 0)
+
+
+def close_shelves(work_x, dim_k):
+    kept_arr = list(work_x.shape[1:])
+    kept_arr[dim_k] *= work_x.shape[0]
+    return jnp.moveaxis(work_x, 0, dim_k).reshape(kept_arr)
 
 
 def shifted(array, axis, by):
@@ -98,7 +110,24 @@
         ],
         axis=2,
     ).astype(jnp.bfloat16)
-    gathered = lax.all_to_all(volts, "chan", split_axis=3, concat_axis=0, tiled=True)
+
+    def check_indices_on(slab_in, bus_axis, buf, inp):
+        q_next = lax.axis_size(bus_axis)
+        piece_next = lax.axis_index(bus_axis)
+        local_now, current_arr = (q_next, piece_next)
+        met_up = sectors_trace(slab_in, buf, local_now)
+        nodes = [met_up[current_arr]]
+        for ii in [*range(1, local_now)]:
+            earlier = met_up[current_arr ^ ii]
+            parts_out = lax.ppermute(
+                earlier, axis_name=bus_axis, perm=[(idx, idx ^ ii) for idx in range(local_now)]
+            )
+            nodes.append(parts_out)
+        u1 = jnp.stack(nodes, axis=0)
+        met_up = u1[current_arr ^ jnp.arange(local_now)]
+        return close_shelves(met_up, inp)
+
+    gathered = check_indices_on(volts, "chan", 3, 0)
     items = gathered.shape[1]
     chan_dev = gathered.shape[3]
     grid = gathered.reshape(side_x, side_y, items, 2, chan_dev)

time: 1560 us -> 1630 us (1.045)
  blocking collectives: 325 us -> 0 us
  waiting for transfers between devices: 245 us -> 543 us
  local copies, waits for them, and re-layouts: 392 us -> 471 us
    all_to_all x1 -> x0, blocking collectives: 325 us -> none  [on_device(): lax.all_to_all(volts, 'chan', split_axis=3, concat_axis=0, tiled=True)]
    ppermute x2, waiting for transfers between devices: 77.6 us -> 210 us  [shifted(): return lax.ppermute(array, axis, pairs)]
    ppermute x0 -> x7, waiting for transfers between devices: none -> 123 us  [check_indices_on(): lax.ppermute(earlier, axis_name=bus_axis, perm=[(idx, idx ^ ii) for idx i...]
    another operation x0 -> x9, local copies, waits for them, and re-layouts: none -> 83.5 us
    reduce_scatter x1, waiting for transfers between devices: 167 us -> 211 us  [on_device(): lax.psum_scatter(dedisperse(extended, local_delays, spec_dev, trials, sca...]
    all_to_all x1 -> x0, local copies, waits for them, and re-layouts: 25.7 us -> none  [on_device(): lax.all_to_all(volts, 'chan', split_axis=3, concat_axis=0, tiled=True)]
    gather x0 -> x3, local copies, waits for them, and re-layouts: none -> 22.2 us  [check_indices_on(): met_up = u1[current_arr ^ jnp.arange(local_now)]]
    unnamed x17 -> x35, local copies, waits for them, and re-layouts: 25.7 us -> 43.6 us
  transfers between devices with their start and end apart: 3 -> 10, of which waited for: 3 -> 7; matrix products, arithmetic and copies ran while one was open for 0% -> 1% of each run, Pallas kernels for 0% -> 0%
where the time goes in v1:
time: 1630 us; the launch traced here: 1620 us
  waiting for transfers between devices  543 us (33%)
  matrix products  476 us (29%)
  local copies, waits for them, and re-layouts  471 us (29%)
  other arithmetic  90.5 us (6%)
  starting transfers between devices  22.8 us (1%)
    reduce_scatter x1, waiting for transfers between devices, on_device(): lax.psum_scatter(dedisperse(extended, local_delays, spec_dev, trials, sca...  211 us
    ppermute x2, waiting for transfers between devices, shifted(): return lax.ppermute(array, axis, pairs)  210 us
    ppermute x7, waiting for transfers between devices, check_indices_on(): lax.ppermute(earlier, axis_name=bus_axis, perm=[(idx, idx ^ ii) for idx i...  123 us
    another operation x2, local copies, waits for them, and re-layouts, transform(): shaped = frames_rows.reshape(rows_count, first, second)  103 us
    another operation x8, local copies, waits for them, and re-layouts  83.3 us
    dot_general x9, matrix products, turn(): jnp.einsum('scb,tc->bst', piece, selector, preferred_element_type=jnp.flo...  82.9 us
    dot_general x1, matrix products, transform(): section_real = jnp.einsum('rab,ak->rkb', shaped, cos_one, precision=highest)  54.9 us
    add x1, other arithmetic, on_device(): filtered + fir_taps[tap_index][None, None, :] * extended_frames[:, offset...  53 us
  transfers between devices with their start and end apart: 10, of which 7 were waited for; matrix products, arithmetic and copies ran while one was open for 1% of the time, Pallas kernels for 0%

profile of v1, /device:TPU:0, one launch (start us, length us, event | category | flops | bytes accessed | tf_op | source)
XLA Modules:
  0.0 1616.8 jit_solution(15391788637939578460)
XLA Ops:
  6.5 22.5 %copy.63 = bf16[256,32768]{0,1:T(8,128)(2,1)} copy(bf16[256,32768]{1,0:T(8,128)(2,1)} %param.7) | data formatting | bytes 33554432 | tf_op args[0]
  29.0 13.1 slice.92
  42.1 19.3 %copy.64 = bf16[256,7,4096]{2,0,1:T(8,128)(2,1)} copy(bf16[256,7,4096]{0,2,1:T(8,128)(2,1)} %slice.92) | data formatting | bytes 29360128 | tf_op jit(solution)/shard_map/slice | solution.py:96
  69.3 16.7 %collective-permute-done = bf16[256,7,4096]{2,0,1:T(8,128)(2,1)} collective-permute-done((bf16[256,7,4096]{2,0,1:T(8,128)(2,1)}, bf16[256,7,4096]{2,0,1:T(8,128)(2,1)}, u32[]{:S(2)}, u32[]{:S(2)}) %collective-permute-start) | collective-permute-done | bytes 14680096 | tf_op jit(solution)/shard_map/ppermute | solution.py:23
  86.0 19.3 %copy.65 = bf16[256,7,4096]{0,2,1:T(8,128)(2,1)} copy(bf16[256,7,4096]{2,0,1:T(8,128)(2,1)} %collective-permute-done) | data formatting | bytes 29360128 | tf_op jit(solution)/shard_map/ppermute | solution.py:23
  105.3 53.0 %multiply_add_fusion = f32[256,8,4096]{0,2,1:T(8,128)} fusion(bf16[256,8,4096]{0,2,1:T(8,128)(2,1)} %bitcast.151, bf16[256,7,4096]{0,2,1:T(8,128)(2,1)} %copy.65, f32[4096]{0:T(1024)S(1)} %bitcast.166, f32[4096]{0:T(1024)S(1)} %bitcast.167, f32[4096]{0:T(1024)S(1)} %bitcast.161, f32[4096]{0:T(1024)S(1)} %bitcast.162, f32[4096]{0:T(1024)S(1)} %bitcast.163, ...), kind=kLoop, calls=%fused_computation.23 | loop fusion | flops 251658240 | bytes 65142784 | tf_op jit(solution)/shard_map/add | solution.py:101
  158.3 32.0 %copy.66 = f32[256,8,4096]{2,1,0:T(8,128)} copy(f32[256,8,4096]{0,2,1:T(8,128)} %multiply_add_fusion) | data formatting | bytes 67108864 | tf_op jit(solution)/shard_map/add | solution.py:101
  190.3 52.6 %reshape_reshape.6 = f32[2048,64,64]{2,1,0:T(8,128)} reshape(f32[256,8,4096]{2,1,0:T(8,128)} %copy.66) | data formatting | bytes 67108864 | tf_op jit(solution)/shard_map/reshape;reshape | solution.py:38
  242.9 50.8 %copy.67 = f32[2048,64,64]{0,1,2:T(8,128)} copy(f32[2048,64,64]{2,1,0:T(8,128)} %reshape_reshape.6) | data formatting | bytes 67108864 | tf_op jit(solution)/shard_map/reshape;reshape | solution.py:38
  293.8 37.0 %fusion.44 = f32[64,2048,64]{1,0,2:T(8,128)} fusion(f32[2048,64,64]{0,1,2:T(8,128)} %copy.67), kind=kOutput, calls=%fused_computation.88 | convolution fusion | flops 6442508288 | bytes 67108864 | tf_op jit(solution)/shard_map/rab,ak->rkb/dot_general | solution.py:42
  330.8 54.9 %add_bitcast_fusion = (f32[2048,64,64]{0,1,2:T(8,128)}, f32[2048,64,64]{0,1,2:T(8,128)}) fusion(f32[64,2048,64]{1,0,2:T(8,128)} %fusion.44, f32[64,64]{0,1:T(8,128)S(1)} %get-tuple-element.144, f32[64,64]{0,1:T(8,128)S(1)} %get-tuple-element.145, f32[2048,64,64]{0,1,2:T(8,128)} %copy.67), kind=kOutput, calls=%fused_computation.22 | convolution fusion | flops 6501228544 | bytes 134250496 | tf_op jit(solution)/shard_map/rab,ak->rkb/dot_general | solution.py:41
  385.6 46.2 %fusion.8 = f32[32,2048,64]{1,0,2:T(8,128)} fusion(f32[2048,64,64]{0,1,2:T(8,128)} %get-tuple-element.121), kind=kOutput, calls=%fused_computation.24 | convolution fusion | flops 3221254144 | bytes 50331648 | tf_op jit(solution)/shard_map/rkb,bm->rmk/dot_general | solution.py:50
  431.8 46.0 %fusion.10 = f32[32,2048,64]{1,0,2:T(8,128)} fusion(f32[2048,64,64]{0,1,2:T(8,128)} %get-tuple-element.121), kind=kOutput, calls=%fused_computation.26 | convolution fusion | flops 3221254144 | bytes 50331648 | tf_op jit(solution)/shard_map/rkb,bm->rmk/dot_general | solution.py:47
  477.8 48.3 %fusion.24 = bf16[2048,32,64]{0,1,2:T(8,128)(2,1)} fusion(f32[32,2048,64]{1,0,2:T(8,128)} %fusion.8, f32[2048,64,64]{0,1,2:T(8,128)} %get-tuple-element.120), kind=kOutput, calls=%fused_computation.49 | convolution fusion | flops 3233837056 | bytes 58720256 | tf_op jit(solution)/shard_map/rkb,bm->rmk/dot_general | solution.py:50
  526.1 29.1 %copy.74 = bf16[2048,32,64]{2,1,0:T(8,128)(2,1)} copy(bf16[2048,32,64]{0,1,2:T(8,128)(2,1)} %fusion.24) | data formatting | bytes 16777216 | tf_op jit(solution)/shard_map/mul | solution.py:56
  555.1 22.8 %mul.342 = bf16[256,8,1,8,256]{4,3,1,0,2:T(8,128)(2,1)} reshape(bf16[2048,32,64]{2,1,0:T(8,128)(2,1)} %copy.74) | data formatting | bytes 16777216 | tf_op jit(solution)/shard_map/mul | solution.py:56
  577.9 49.5 %fusion.23 = bf16[2048,32,64]{0,1,2:T(8,128)(2,1)} fusion(f32[32,2048,64]{1,0,2:T(8,128)} %fusion.10, f32[2048,64,64]{0,1,2:T(8,128)} %get-tuple-element.120), kind=kOutput, calls=%fused_computation.48 | convolution fusion | flops 3233837056 | bytes 58720256 | tf_op jit(solution)/shard_map/rkb,bm->rmk/dot_general | solution.py:47
  627.4 29.2 %copy.71 = bf16[2048,32,64]{2,1,0:T(8,128)(2,1)} copy(bf16[2048,32,64]{0,1,2:T(8,128)(2,1)} %fusion.23) | data formatting | bytes 16777216 | tf_op jit(solution)/shard_map/mul | solution.py:55
  656.6 22.8 %mul.339 = bf16[256,8,1,8,256]{4,3,1,0,2:T(8,128)(2,1)} reshape(bf16[2048,32,64]{2,1,0:T(8,128)(2,1)} %copy.71) | data formatting | bytes 16777216 | tf_op jit(solution)/shard_map/mul | solution.py:55
  679.4 8.3 constant_dynamic-update-slice_fusion.1
  687.7 8.3 constant_dynamic-update-slice_fusion
  695.9 74.0 %constant_dynamic-slice_fusion = (bf16[256,8,2,1,256]{4,3,1,0,2:T(2,128)(2,1)S(1)}, bf16[256,8,2,1,256]{4,3,1,0,2:T(2,128)(2,1)}, bf16[256,8,2,1,256]{4,3,1,0,2:...) fusion(bf16[256,8,2,8,256]{4,3,1,0,2:T(8,128)(2,1)} %constant_d, ...), kind=kLoop, calls=%fused_computation.145 | loop fusion | bytes 33554464 | tf_op jit(solution)/shard_map/dynamic-slice.7
  787.7 11.4 collective-permute-done.1
  803.7 41.4 %collective-permute-done.2 = bf16[256,8,2,256]{3,1,2,0:T(8,128)(2,1)S(1)} collective-permute-done((bf16[256,8,2,256]{3,1,2,0:T(8,128)(2,1)S(1)}, bf16[256,8,2,256]{3,1,2,0:T(8,128)(2,1)S(1)}, u32[]{:S(2)}, u32[]{:S(2)}) %collective-permute-start.2) | collective-permute-done | bytes 2097184 | tf_op jit(solution)/shard_map/ppermute | solution.py:122
  850.4 16.8 %collective-permute-done.3 = bf16[256,8,2,256]{3,1,2,0:T(8,128)(2,1)} collective-permute-done((bf16[256,8,2,256]{3,1,2,0:T(8,128)(2,1)S(1)}, bf16[256,8,2,256]{3,1,2,0:T(8,128)(2,1)}, u32[]{:S(2)}, u32[]{:S(2)}) %collective-permute-start.3) | collective-permute-done | bytes 2097184 | tf_op jit(solution)/shard_map/ppermute | solution.py:122
  870.7 52.8 %collective-permute-done.5 = bf16[256,8,2,256]{3,1,2,0:T(8,128)(2,1)} collective-permute-done((bf16[256,8,2,256]{3,1,2,0:T(8,128)(2,1)S(1)}, bf16[256,8,2,256]{3,1,2,0:T(8,128)(2,1)}, u32[]{:S(2)}, u32[]{:S(2)}) %collective-permute-start.5) | collective-permute-done | bytes 2097184 | tf_op jit(solution)/shard_map/ppermute | solution.py:122
  931.6 8.1 gather_fusion
  947.8 13.7 pad_maximum_fusion.1
  987.9 13.8 fusion.39
  1001.7 16.0 fusion.27
  1017.7 12.3 fusion.29
  1030.0 13.7 fusion.38
  1043.7 16.0 fusion.31
  1059.7 23.4 %fusion.121 = (f32[8,256]{1,0:T(8,128)S(1)}, f32[8,256,64,32]{1,2,3,0:T(8,128)}) fusion(f32[8,256,32,64]{1,3,2,0:T(8,128)} %fusion.29, bf16[8,256,64,32]{1,3,0,2:T(8,128)(2,1)S(1)} %copy-done.4, bf16[2,64,64]{2,1,0:T(8,128)(2,1)S(1)} %copy-done.11, f32[8,256,32,64]{1,3,2,0:T(8,128)} %fusion.31, f32[8,256,32,64]{1,3,2,0:T(8,128)} %fusion.27), kind=kOutput, calls=%fused_computation.177 | convolution fusion | flops 562034688 | bytes 75522048 | tf_op jit(solution)/shard_map/qx,ncxp->ncqp/dot_general | solution.py:66
  1083.0 15.2 copy.89
  1104.5 193.1 %collective-permute-done.8 = bf16[8,256,2048]{1,2,0:T(8,128)(2,1)} collective-permute-done((bf16[8,256,2048]{1,2,0:T(8,128)(2,1)}, bf16[8,256,2048]{1,2,0:T(8,128)(2,1)}, u32[]{:S(2)}, u32[]{:S(2)}) %collective-permute-start.8) | collective-permute-done | bytes 8388640 | tf_op jit(solution)/shard_map/ppermute | solution.py:23
  1297.6 13.7 pad_maximum_fusion.2
  1311.3 82.9 %while.14 = (s32[]{:T(128)}, f32[2048,8,64]{0,2,1:T(8,128)}, s32[64,256]{1,0:T(8,128)S(1)}, bf16[16,256,2048]{1,2,0:T(8,128)(2,1)}, s32[]{:T(128)}, /*index=5*/s32[]{:T(128)}) while((s32[]{:T(128)}, f32[2048,8,64]{0,2,1:T(8,128)}, s32[64,256]{1,0:T(8,128)S(1)}, bf16[16,256,2048]{1,2,0:T(8,128)(2,1)}, s32[]{:T(128)}, ...), condition=%wide.region_2.3_spmd.clone, body=%wide.region_1.2_spmd.clone.sunk | while | flops 538984448 | bytes 16843852 | solution.py:82
  1311.3 8.1 bitcast_add_fusion.2
  1319.4 9.5 bitcast_add_fusion.2
  1328.9 9.5 bitcast_add_fusion.2
  1338.4 9.5 bitcast_add_fusion.2
  1347.9 9.3 bitcast_add_fusion.2
  1357.2 9.3 bitcast_add_fusion.2
  1366.4 9.3 bitcast_add_fusion.2
  1375.7 9.3 bitcast_add_fusion.2
  1385.0 9.3 bitcast_add_fusion.2
  1399.2 210.5 %reduce-scatter.2.cloned.1.call-done = f32[256,8,64]{0,2,1:T(8,128)} async-done(((f32[2048,8,64]{0,2,1:T(8,128)}), f32[256,8,64]{0,2,1:T(8,128)}) %reduce-scatter.2.cloned.1.call-update) | async-done | bytes 524304 | tf_op jit(solution)/shard_map/reduce_scatter | solution.py:149
  (69 shorter events, 92.4 us)
Async XLA Ops:
  6.5 1097.9 %copy-start = (s32[64,2048]{1,0:T(8,128)S(1)}, s32[64,2048]{1,0:T(8,128)}, u32[]{:S(2)}) copy-start(s32[64,2048]{1,0:T(8,128)} %param.11) | copy-start | bytes 1572868
  6.5 1603.2 %reduce-scatter.2.cloned.1.call-start = ((), (), s32[]{:S(2)}) async-start(), calls=%async_computation.1 | async-start | bytes 4718592 | tf_op jit(solution)/shard_map/reduce_scatter | solution.py:149
  42.1 27.0 %copy-start.10 = (f32[8,4096]{1,0:T(8,128)S(1)}, f32[8,4096]{1,0:T(8,128)}, u32[]{:S(2)}) copy-start(f32[8,4096]{1,0:T(8,128)} %param.8) | copy-start | bytes 393220
  61.5 24.5 %collective-permute-start = (bf16[256,7,4096]{2,0,1:T(8,128)(2,1)}, bf16[256,7,4096]{2,0,1:T(8,128)(2,1)}, u32[]{:S(2)}, u32[]{:S(2)}) collective-permute-start(bf16[256,7,4096]{2,0,1:T(8,128)(2,1)} %copy.64), channel_id=1, source_target_pairs={{0,1},{1,2},{2,3},{4,5},{5,6},{6,7},{8,9},{9,10},{10,11},{12,13},{... | collective-permute-start | bytes 44040200 | tf_op jit(solution)/shard_map/ppermute | solution.py:23
  770.0 12.7 copy-start.7
  770.0 16.2 copy-start.6
  770.0 17.3 %copy-start.5 = (bf16[256,8,2,1,256]{4,3,1,0,2:T(2,128)(2,1)S(1)}, bf16[256,8,2,1,256]{4,3,1,0,2:T(2,128)(2,1)}, u32[]{:S(2)}) copy-start(bf16[256,8,2,1,256]{4,3,1,0,2:T(2,128)(2,1)} %get-tuple-element.127) | copy-start | bytes 6291460
  772.7 26.4 %collective-permute-start.1 = (bf16[256,8,2,256]{3,1,2,0:T(8,128)(2,1)S(1)}, bf16[256,8,2,256]{3,1,2,0:T(8,128)(2,1)S(1)}, u32[]{:S(2)}, u32[]{:S(2)}) collective-permute-start(bf16[256,8,2,256]{3,1,2,0:T(8,128)(2,1)S(1)} %bitcast.159), channel_id=1, source_target_pairs={{0,4},{4,0},{8,12},{12,8},{16,20},{20,16},{24,28},{28,24},{1,5},{5... | collective-permute-start | bytes 6291464 | tf_op jit(solution)/shard_map/ppermute | solution.py:122
  777.6 67.5 %collective-permute-start.2 = (bf16[256,8,2,256]{3,1,2,0:T(8,128)(2,1)S(1)}, bf16[256,8,2,256]{3,1,2,0:T(8,128)(2,1)S(1)}, u32[]{:S(2)}, u32[]{:S(2)}) collective-permute-start(bf16[256,8,2,256]{3,1,2,0:T(8,128)(2,1)S(1)} %bitcast.158), channel_id=1, source_target_pairs={{0,8},{4,12},{8,0},{12,4},{16,24},{20,28},{24,16},{28,20},{1,9},{5... | collective-permute-start | bytes 6291464 | tf_op jit(solution)/shard_map/ppermute | solution.py:122
  782.4 84.8 %collective-permute-start.3 = (bf16[256,8,2,256]{3,1,2,0:T(8,128)(2,1)S(1)}, bf16[256,8,2,256]{3,1,2,0:T(8,128)(2,1)}, u32[]{:S(2)}, u32[]{:S(2)}) collective-permute-start(bf16[256,8,2,256]{3,1,2,0:T(8,128)(2,1)S(1)} %bitcast.156), channel_id=1, source_target_pairs={{0,12},{4,8},{8,4},{12,0},{16,28},{20,24},{24,20},{28,16},{1,13},{... | collective-permute-start | bytes 6291464 | tf_op jit(solution)/shard_map/ppermute | solution.py:122
  783.0 86.0 %collective-permute-start.4 = (bf16[256,8,2,256]{3,1,2,0:T(8,128)(2,1)S(1)}, bf16[256,8,2,256]{3,1,2,0:T(8,128)(2,1)}, u32[]{:S(2)}, u32[]{:S(2)}) collective-permute-start(bf16[256,8,2,256]{3,1,2,0:T(8,128)(2,1)S(1)} %bitcast.155), channel_id=1, source_target_pairs={{0,16},{4,20},{8,24},{12,28},{16,0},{20,4},{24,8},{28,12},{1,17},{... | collective-permute-start | bytes 6291464 | tf_op jit(solution)/shard_map/ppermute | solution.py:122
  786.5 137.0 %collective-permute-start.5 = (bf16[256,8,2,256]{3,1,2,0:T(8,128)(2,1)S(1)}, bf16[256,8,2,256]{3,1,2,0:T(8,128)(2,1)}, u32[]{:S(2)}, u32[]{:S(2)}) collective-permute-start(bf16[256,8,2,256]{3,1,2,0:T(8,128)(2,1)S(1)} %bitcast.154), channel_id=1, source_target_pairs={{0,20},{4,16},{8,28},{12,24},{16,4},{20,0},{24,12},{28,8},{1,21},{... | collective-permute-start | bytes 6291464 | tf_op jit(solution)/shard_map/ppermute | solution.py:122
  799.1 47.0 %copy-start.8 = (bf16[256,8,2,256]{3,1,2,0:T(8,128)(2,1)}, bf16[256,8,2,256]{3,1,2,0:T(8,128)(2,1)S(1)}, u32[]{:S(2)}) copy-start(bf16[256,8,2,256]{3,1,2,0:T(8,128)(2,1)S(1)} %collective-permute-done.1) | copy-start | bytes 6291460
  799.1 126.2 %collective-permute-start.6 = (bf16[256,8,2,256]{3,1,2,0:T(8,128)(2,1)S(1)}, bf16[256,8,2,256]{3,1,2,0:T(8,128)(2,1)S(1)}, u32[]{:S(2)}, u32[]{:S(2)}) collective-permute-start(bf16[256,8,2,256]{3,1,2,0:T(8,128)(2,1)S(1)} %bitcast.153), channel_id=1, source_target_pairs={{0,24},{4,28},{8,16},{12,20},{16,8},{20,12},{24,0},{28,4},{1,25},{... | collective-permute-start | bytes 6291464 | tf_op jit(solution)/shard_map/ppermute | solution.py:122
  845.1 1.4 copy-start.9
  845.1 80.3 %collective-permute-start.7 = (bf16[256,8,2,256]{3,1,2,0:T(8,128)(2,1)S(1)}, bf16[256,8,2,256]{3,1,2,0:T(8,128)(2,1)S(1)}, u32[]{:S(2)}, u32[]{:S(2)}) collective-permute-start(bf16[256,8,2,256]{3,1,2,0:T(8,128)(2,1)S(1)} %bitcast.157), channel_id=1, source_target_pairs={{0,28},{4,24},{8,20},{12,16},{16,12},{20,8},{24,4},{28,0},{1,29},{... | collective-permute-start | bytes 6291464 | tf_op jit(solution)/shard_map/ppermute | solution.py:122
  961.5 10.3 copy-start.12
  968.5 3.2 copy-start.2
  968.6 11.3 copy-start.1
  987.9 13.8 copy-start.11
  1001.7 16.0 copy-start.3
  1043.7 16.0 copy-start.4
  1103.2 194.4 %collective-permute-start.8 = (bf16[8,256,2048]{1,2,0:T(8,128)(2,1)}, bf16[8,256,2048]{1,2,0:T(8,128)(2,1)}, u32[]{:S(2)}, u32[]{:S(2)}) collective-permute-start(bf16[8,256,2048]{1,2,0:T(8,128)(2,1)} %fusion.22), channel_id=1, source_target_pairs={{1,0},{2,1},{3,2},{5,4},{6,5},{7,6},{9,8},{10,9},{11,10},{13,12},{... | collective-permute-start | bytes 25165832 | tf_op jit(solution)/shard_map/ppermute | solution.py:23
Sparse Core Ops, SparseCore 0:
  1399.3 210.3 reduce-scatter.1
